TPU v7x, 32 devices: a whole 2x2x4 slice. The times are simulated.
32 devices in a mesh: groups: 2 (over x), psg: 16 (over z, y, core).
Axes of the slice: x: 2, y: 2, z: 4, core: 2. Of those that a mesh axis runs over, the one named last changes fastest.
Arguments:
- queries: bfloat16 [64, 32, 128], P(('groups', 'psg')), parts along dimension 0, may hold values from -0.29882812 to 0.29882812
- candidates: int32 [64, 512], P(('groups', 'psg')), parts along dimension 0, may hold values from 0 to 159
- centroids: bfloat16 [8192, 128], P('psg'), may hold values from -6 to 6
- bucket_weights: float32 [4, 128], replicated, may hold values from -1 to 1
- centroid_shard: int32 [32768, 1], P('psg'), may hold values from 0 to 15; in each aligned block of 2048 rows (0 to 2047, 2048 to 4095, ...) at most 256 rows name the same one
- centroid_row: int32 [32768], P('psg'), may hold values from 0 to 511
- residual_codes: int32 [32768, 128], P('psg'), may hold values from 0 to 3
- tile_count: int32 [160], replicated, may hold values from 1 to 3, 256 in all
- last_fill: int32 [160], replicated, may hold values from 1 to 128
Outputs:
- scores: float32 [64, 512], P(('groups', 'psg')), parts along dimension 0
There are 2 independent parts, one for each index of `groups`. A program takes and returns all parts, laid end to end along the dimension named above; an argument that names none is the same for every part. Nothing has to cross between parts.
Inputs may be any that keep to these rules, and one draw needn't show every extreme that they name: `tile_count`: tiles are numbered along psg, device k holding tiles k * 16 onward; the counts sum to 256, so a passage may continue on the next device. `centroid_shard`: among the 2048 token slots of one device, at most 256 name the same device; on some device some value is named exactly 256 times.
All inputs are finite; a program needn't handle non-finite values.
Results may differ from a plain program's by a relative error of at most 0.0003.
Values may be sent and summed in bfloat16 or wider, within the bound.
No kernel may reach another device: no remote copies, remote signals or barrier semaphores. Data moves between devices by JAX's collectives and lax.ppermute only.
A program may use at most 64 MiB of HBM per device.

v0:
```python
import jax
import jax.numpy as jnp
from jax import lax
from jax.sharding import PartitionSpec as P

TILE = 128
epsilon = 1e-06


def tile_layout(tile_count, last_fill, total_tiles, tile_len):
    starts = jnp.cumsum(tile_count) - tile_count
    last_tile = starts + tile_count - 1
    tile_fill = jnp.full((total_tiles,), tile_len, jnp.int32).at[last_tile].set(last_fill)
    return (starts, tile_fill)


def decode(picked, residual_codes, bucket_weights):
    residual = jnp.zeros(residual_codes.shape, jnp.float32)
    for bucket in range(4):
        residual = residual + jnp.where(
            residual_codes == bucket, bucket_weights[bucket][None, :], jnp.float32(0.0)
        )
    summed = picked.astype(jnp.float32) + residual
    scale = lax.rsqrt(jnp.sum(summed * summed, axis=1, keepdims=True) + epsilon)
    return (summed * scale).astype(jnp.bfloat16)


def assemble(own_maxima, candidates, starts, total_tiles, query_len):
    num_queries, num_cand = candidates.shape
    marker = jnp.zeros((total_tiles,), jnp.int32).at[starts].add(1)
    owner_id = jnp.cumsum(marker)
    same_next = jnp.concatenate([owner_id[1:] == owner_id[:-1], jnp.zeros((1,), bool)])
    same_after = jnp.concatenate([owner_id[2:] == owner_id[:-2], jnp.zeros((2,), bool)])
    shifted_one = jnp.concatenate([own_maxima[:, 1:], own_maxima[:, :1]], axis=1)
    shifted_two = jnp.concatenate([own_maxima[:, 2:], own_maxima[:, :2]], axis=1)
    combined = jnp.maximum(own_maxima, jnp.where(same_next[None, :], shifted_one, own_maxima))
    combined = jnp.maximum(combined, jnp.where(same_after[None, :], shifted_two, own_maxima))
    combined = combined.reshape(num_queries, query_len, total_tiles)
    first_tile = starts[candidates]
    selector = (
        first_tile[:, :, None] == jnp.arange(total_tiles, dtype=jnp.int32)[None, None, :]
    ).astype(jnp.float32)
    return jnp.einsum(
        "qit,qct->qc",
        combined,
        selector,
        precision=lax.Precision.HIGHEST,
        preferred_element_type=jnp.float32,
    )


def per_device(
    queries,
    candidates,
    centroids,
    bucket_weights,
    centroid_shard,
    centroid_row,
    residual_codes,
    tile_count,
    last_fill,
):
    n_psg = lax.axis_size("psg")
    shard_index = lax.axis_index("psg")
    tok_dev = residual_codes.shape[0]
    tiles_dev = tok_dev // TILE
    cent_dev = centroids.shape[0]
    owners = centroid_shard[:, 0]
    codebook = lax.all_gather(centroids, "psg", axis=0, tiled=True)
    picked = jnp.take(codebook, owners * cent_dev + centroid_row, axis=0)
    embedded = decode(picked, residual_codes, bucket_weights)
    total_tiles = tiles_dev * n_psg
    starts, tile_fill = tile_layout(tile_count, last_fill, total_tiles, TILE)
    local_fill = lax.dynamic_slice_in_dim(tile_fill, shard_index * tiles_dev, tiles_dev, 0)
    token_mask = jnp.arange(TILE, dtype=jnp.int32)[None, :] < local_fill[:, None]
    pad_bias = jnp.where(token_mask, jnp.float32(0.0), -jnp.inf).reshape(-1)
    per_block = max(1, 512 // TILE)
    while tiles_dev % per_block:
        per_block -= 1
    width = per_block * TILE
    piece = lax.all_gather(queries, "psg", axis=0, tiled=True)
    flat_rows = piece.reshape(-1, piece.shape[-1])
    pieces = []
    for block in range(tiles_dev // per_block):
        key_block = embedded[block * width : (block + 1) * width]
        block_scores = jnp.einsum(
            "qd,kd->qk", flat_rows, key_block, preferred_element_type=jnp.float32
        )
        block_scores = block_scores + pad_bias[block * width : (block + 1) * width][None, :]
        pieces.append(jnp.max(block_scores.reshape(flat_rows.shape[0], per_block, TILE), axis=2))
    maxima = jnp.concatenate(pieces, axis=1)
    own_maxima = lax.all_to_all(maxima, "psg", split_axis=0, concat_axis=1, tiled=True)
    return assemble(own_maxima, candidates, starts, total_tiles, queries.shape[1])


def solution(mesh):
    placed = (
        P(("groups", "psg"), None, None),
        P(("groups", "psg"), None),
        P("psg", None),
        P(),
        P("psg", None),
        P("psg"),
        P("psg", None),
        P(),
        P(),
    )
    return jax.shard_map(
        per_device,
        mesh=mesh,
        in_specs=placed,
        out_specs=P(("groups", "psg"), None),
        check_vma=False,
    )
```

profile of v0, /device:TPU:0, one launch (start us, length us, event | category | flops | bytes accessed | tf_op | source)
XLA Modules:
  0.0 90.6 jit_solution(17494278856567617430)
XLA Ops:
  6.5 0.7 all-gather.2.cloned.1.call-update
  7.3 0.7 pad_bitcast_fusion
  8.6 0.7 compare_select_fusion.2
  9.2 1.7 %scatter_custom_fusion.1 = s32[256]{0:T(256)S(1)} fusion(s32[160]{0:T(256)S(1)} %get-tuple-element.5, s32[160]{0:T(256)S(1)} %broadcast.58, s32[]{:T(128)} %constant.21.clone.1), kind=kCustom, calls=%fused_computation.54 | custom fusion | flops 160 | bytes 1028 | tf_op jit(solution)/shard_map/scatter-add | solution.py:30
  11.3 0.7 fusion.9
  12.0 1.2 %scatter_custom_fusion = s32[256]{0:T(256)S(1)} fusion(s32[160]{0:T(256)S(1)} %get-tuple-element.17, s32[160]{0:T(256)} %param.17, s32[]{:T(128)} %constant.15.clone.1), kind=kCustom, calls=%fused_computation.56 | custom fusion | bytes 1536 | tf_op jit(solution)/shard_map/scatter | solution.py:13
  13.5 24.3 %all_gather.7 = bf16[32,32,128]{2,1,0:T(8,128)(2,1)S(1)} all-gather(bf16[2,32,128]{2,1,0:T(8,128)(2,1)} %param.9), channel_id=1, replica_groups=mesh['groups'=2,'psg'=16] {'psg'}, dimensions={0}, use_global_device_ids=true | all-gather | bytes 278528 | tf_op jit(solution)/shard_map/all_gather | solution.py:81
  38.0 0.8 slice_bitcast_fusion.7
  38.9 0.7 broadcast_multiply_fusion
  39.6 0.7 compare_and_fusion
  40.3 0.7 broadcast_clamp_fusion
  41.0 13.0 %all-gather.2.cloned.1.call-done = bf16[8192,128]{1,0:T(8,128)(2,1)} async-done(((bf16[512,128]{1,0:T(8,128)(2,1)}), bf16[8192,128]{1,0:T(8,128)(2,1)}) %all-gather.2.cloned.1.call-update) | async-done | bytes 2097168 | tf_op jit(solution)/shard_map/all_gather | solution.py:69
  54.0 7.5 %gather_fusion = bf16[2048,128]{1,0:T(8,128)(2,1)S(1)} fusion(bf16[8192,128]{1,0:T(8,128)(2,1)} %all-gather.2.cloned.1.call-done, s32[2048]{0:T(1024)S(1)} %broadcast_clamp_fusion), kind=kCustom, calls=%fused_computation | custom fusion | bytes 1056768 | tf_op jit(solution)/shard_map/jit(_take)/gather | solution.py:70
  61.5 0.9 multiply_reduce_fusion
  63.2 0.5 bitcast_reduce_fusion.2
  63.7 0.5 bitcast_reduce_fusion.1
  64.8 0.7 reshape.153
  65.5 3.5 %all-to-all-start = ((f32[16,1,1024]{2,1,0:T(1,128)}), f32[16,1,1024]{2,1,0:T(1,128)S(1)}, u32[]{:S(2)}, u32[]{:S(2)}) async-start(f32[16,1,1024]{2,1,0:T(1,128)} %reshape.153), calls=%async_computation | async-start | bytes 131072 | tf_op jit(solution)/shard_map/all_to_all | solution.py:92
  69.1 6.8 %gather_fusion.1 = s32[1024]{0:T(1024)S(1)} fusion(s32[160]{0:T(256)S(1)} %get-tuple-element.6, s32[1024]{0:T(1024)S(1)} %broadcast_clamp_fusion.1), kind=kCustom, calls=%fused_computation.1 | custom fusion | bytes 12288 | tf_op jit(solution)/shard_map/gather | solution.py:39
  76.0 0.5 broadcast.78
  76.6 0.8 reduce.8
  78.4 4.0 %fusion.3 = f32[2,256]{0,1:T(8,128)S(1)} fusion(f32[2,32,256]{1,0,2:T(2,128)S(1)} %all_to_all.19, f32[2,32,1]{1,0,2:T(2,128)S(1)} %concatenate.28, f32[2,32,255]{1,0,2:T(2,128)S(1)} %copy.29, f32[2,32,2]{1,0,2:T(2,128)S(1)} %concatenate.32, f32[2,32,254]{1,0,2:T(2,128)S(1)} %copy.31, pred[256]{0:T(512)(128)(4,1)S(1)} %concatenate.30, ...), kind=kLoop, calls=%fused_computation.20 | loop fusion | flops 114176 | bytes 199168 | tf_op jit(solution)/shard_map/qit,qct->qc/reduce_sum | solution.py:43
  82.5 0.6 fusion
  83.1 0.6 copy.37
  (46 shorter events, 4.1 us)
Async XLA Ops:
  6.5 47.5 %all-gather.2.cloned.1.call-start = ((), (), s32[]{:S(2)}) async-start(), calls=%async_computation.1 | async-start | bytes 2228224 | tf_op jit(solution)/shard_map/all_gather | solution.py:69
  41.0 20.5 %copy-start = (s32[2048,128]{1,0:T(8,128)S(1)}, s32[2048,128]{1,0:T(8,128)}, u32[]{:S(2)}) copy-start(s32[2048,128]{1,0:T(8,128)} %param.15) | copy-start | bytes 3145732
  65.5 10.5 %all-to-all-start = ((f32[16,1,1024]{2,1,0:T(1,128)}), f32[16,1,1024]{2,1,0:T(1,128)S(1)}, u32[]{:S(2)}, u32[]{:S(2)}) async-start(f32[16,1,1024]{2,1,0:T(1,128)} %reshape.153), calls=%async_computation | async-start | bytes 131072 | tf_op jit(solution)/shard_map/all_to_all | solution.py:92
Sparse Core Ops, SparseCore 0:
  9.5 44.4 all-gather.1
where the time goes:
time: 91.1 us; the launch traced here: 90.6 us
  blocking collectives  24.3 us (27%)
  local copies, waits for them, and re-layouts  20.6 us (23%)
  waiting for transfers between devices  13.8 us (15%)
  between operations  13.6 us (15%)
  other arithmetic  12.4 us (14%)
  starting transfers between devices  3.5 us (4%)
  matrix products  2.45 us (3%)
    all_gather x1, blocking collectives, per_device(): piece = lax.all_gather(queries, 'psg', axis=0, tiled=True)  24.3 us
    all_gather x1, waiting for transfers between devices, per_device(): codebook = lax.all_gather(centroids, 'psg', axis=0, tiled=True)  13 us
    gather x1, local copies, waits for them, and re-layouts, per_device(): picked = jnp.take(codebook, owners * cent_dev + centroid_row, axis=0)  7.45 us
    gather x2, local copies, waits for them, and re-layouts, assemble(): first_tile = starts[candidates]  6.83 us
    reduce_sum x1, other arithmetic, assemble(): jnp.einsum('qit,qct->qc', combined, selector, precision=lax.Precision.HIG...  4.02 us
    all_to_all x1, starting transfers between devices, per_device(): lax.all_to_all(maxima, 'psg', split_axis=0, concat_axis=1, tiled=True)  3.5 us
    dot_general x4, matrix products, per_device(): jnp.einsum('qd,kd->qk', flat_rows, key_block, preferred_element_type=jnp....  1.83 us
  transfers between devices with their start and end apart: 2, of which 1 were waited for; matrix products, arithmetic and copies ran while one was open for 18% of the time, Pallas kernels for 0%

commit v1 on v0

--- a/solution.py
+++ b/solution.py
@@ -2,6 +2,7 @@
 import jax.numpy as jnp
 from jax import lax
 from jax.sharding import PartitionSpec as P
+from jax.lax import axis_index, axis_size, ppermute
 
 TILE = 128
 epsilon = 1e-06
@@ -78,7 +79,16 @@
     while tiles_dev % per_block:
         per_block -= 1
     width = per_block * TILE
-    piece = lax.all_gather(queries, "psg", axis=0, tiled=True)
+    nd = axis_size("psg")
+    in_order = [(dev_i, (dev_i + 1) % nd) for dev_i in range(nd)]
+    so_far_all = [(dev_i, (dev_i - 1) % nd) for dev_i in range(nd)]
+    p_next, right_arr = ([queries], [queries])
+    for _ in range(nd // 2):
+        p_next.append(ppermute(p_next[-1], axis_name="psg", perm=in_order))
+    for _ in range((nd - 1) // 2):
+        right_arr.append(ppermute(right_arr[-1], "psg", so_far_all))
+    then = jnp.concatenate([*p_next[::-1], *right_arr[1:]], 0)
+    piece = jnp.roll(then, (axis_index("psg") - nd // 2) * queries.shape[0], 0)
     flat_rows = piece.reshape(-1, piece.shape[-1])
     pieces = []
     for block in range(tiles_dev // per_block):

time: 91.1 us -> 102 us (1.12)
  starting transfers between devices: 3.5 us -> 38 us
  blocking collectives: 24.3 us -> 0 us
  local copies, waits for them, and re-layouts: 20.6 us -> 22.4 us
    ppermute x0 -> x15, starting transfers between devices: none -> 32.2 us  [the longest x7 31.7 us: per_device(): right_arr.append(ppermute(right_arr[-1], 'psg', so_far_all))]
    all_gather x1 -> x0, blocking collectives: 24.3 us -> none  [per_device(): piece = lax.all_gather(queries, 'psg', axis=0, tiled=True)]
    all_gather x1, waiting for transfers between devices: 13 us -> 0.02 us  [per_device(): codebook = lax.all_gather(centroids, 'psg', axis=0, tiled=True)]
    ppermute x0 -> x15, waiting for transfers between devices: none -> 12.7 us  [the longest x8 8.32 us: per_device(): p_next.append(ppermute(p_next[-1], axis_name='psg', perm=in_order))]
    all_to_all x1, starting transfers between devices: 3.5 us -> 5.8 us  [per_device(): lax.all_to_all(maxima, 'psg', split_axis=0, concat_axis=1, tiled=True)]
    unnamed x5 -> x36, local copies, waits for them, and re-layouts: 0.84 us -> 2.54 us
  transfers between devices with their start and end apart: 2 -> 17, of which waited for: 1 -> 11; matrix products, arithmetic and copies ran while one was open for 18% -> 18% of each run, Pallas kernels for 0% -> 0%
where the time goes in v1:
time: 102 us
  starting transfers between devices  38 us (37%)
  local copies, waits for them, and re-layouts  22.4 us (22%)
  between operations  13.7 us (13%)
  waiting for transfers between devices  12.8 us (13%)
  other arithmetic  12.4 us (12%)
  matrix products  2.44 us (2%)
    ppermute x7, starting transfers between devices, per_device(): right_arr.append(ppermute(right_arr[-1], 'psg', so_far_all))  31.7 us
    ppermute x8, waiting for transfers between devices, per_device(): p_next.append(ppermute(p_next[-1], axis_name='psg', perm=in_order))  8.32 us
    gather x1, local copies, waits for them, and re-layouts, per_device(): picked = jnp.take(codebook, owners * cent_dev + centroid_row, axis=0)  7.55 us
    gather x2, local copies, waits for them, and re-layouts, assemble(): first_tile = starts[candidates]  6.86 us
    all_to_all x1, starting transfers between devices, per_device(): lax.all_to_all(maxima, 'psg', split_axis=0, concat_axis=1, tiled=True)  5.8 us
    ppermute x7, waiting for transfers between devices, per_device(): right_arr.append(ppermute(right_arr[-1], 'psg', so_far_all))  4.42 us
    reduce_sum x1, other arithmetic, assemble(): jnp.einsum('qit,qct->qc', combined, selector, precision=lax.Precision.HIG...  4.03 us
    unnamed x36, local copies, waits for them, and re-layouts  2.54 us
  transfers between devices with their start and end apart: 17, of which 11 were waited for; matrix products, arithmetic and copies ran while one was open for 18% of the time, Pallas kernels for 0%

profile of v1, /device:TPU:0, one launch (start us, length us, event | category | flops | bytes accessed | tf_op | source)
XLA Modules:
  0.0 101.8 jit_solution(17796609016214343100)
XLA Ops:
  7.0 5.0 %collective-permute-start.8 = (bf16[2,32,128]{2,1,0:T(8,128)(2,1)}, bf16[2,32,128]{2,1,0:T(8,128)(2,1)S(1)}, u32[]{:S(2)}, u32[]{:S(2)}) collective-permute-start(bf16[2,32,128]{2,1,0:T(8,128)(2,1)} %param.9), channel_id=1, source_target_pairs={{0,15},{1,0},{2,1},{3,2},{4,3},{5,4},{6,5},{7,6},{8,7},{9,8},{10,9... | collective-permute-start | bytes 49160 | tf_op jit(solution)/shard_map/ppermute | solution.py:89
  16.1 1.2 %scatter_custom_fusion = s32[256]{0:T(256)S(1)} fusion(s32[160]{0:T(256)S(1)} %get-tuple-element.17, s32[160]{0:T(256)} %param.17, s32[]{:T(128)} %constant.79.clone.1), kind=kCustom, calls=%fused_computation.88 | custom fusion | bytes 1536 | tf_op jit(solution)/shard_map/scatter | solution.py:14
  17.6 5.9 %collective-permute-done.1 = bf16[2,32,128]{2,1,0:T(8,128)(2,1)S(1)} collective-permute-done((bf16[2,32,128]{2,1,0:T(8,128)(2,1)S(1)}, bf16[2,32,128]{2,1,0:T(8,128)(2,1)S(1)}, u32[]{:S(2)}, u32[]{:S(2)}) %collective-permute-start.1) | collective-permute-done | bytes 16416 | tf_op jit(solution)/shard_map/ppermute | solution.py:87
  24.2 4.5 %collective-permute-start.9 = (bf16[2,32,128]{2,1,0:T(8,128)(2,1)S(1)}, bf16[2,32,128]{2,1,0:T(8,128)(2,1)S(1)}, u32[]{:S(2)}, u32[]{:S(2)}) collective-permute-start(bf16[2,32,128]{2,1,0:T(8,128)(2,1)S(1)} %collective-permute-done.8), channel_id=1, source_target_pairs={{0,15},{1,0},{2,1},{3,2},{4,3},{5,4},{6,5},{7,6},{8,7},{9,8},{10,9... | collective-permute-start | bytes 49160 | tf_op jit(solution)/shard_map/ppermute | solution.py:89
  28.7 0.8 collective-permute-done.2
  30.2 4.5 %collective-permute-start.10 = (bf16[2,32,128]{2,1,0:T(8,128)(2,1)S(1)}, bf16[2,32,128]{2,1,0:T(8,128)(2,1)S(1)}, u32[]{:S(2)}, u32[]{:S(2)}) collective-permute-start(bf16[2,32,128]{2,1,0:T(8,128)(2,1)S(1)} %collective-permute-done.9), channel_id=1, source_target_pairs={{0,15},{1,0},{2,1},{3,2},{4,3},{5,4},{6,5},{7,6},{8,7},{9,8},{10,9... | collective-permute-start | bytes 49160 | tf_op jit(solution)/shard_map/ppermute | solution.py:89
  35.4 0.8 slice_bitcast_fusion.7
  36.2 1.7 %scatter_custom_fusion.1 = s32[256]{0:T(256)S(1)} fusion(s32[160]{0:T(256)S(1)} %get-tuple-element.5, s32[160]{0:T(256)S(1)} %broadcast.55, s32[]{:T(128)} %constant.38.clone.1), kind=kCustom, calls=%fused_computation.86 | custom fusion | flops 160 | bytes 1028 | tf_op jit(solution)/shard_map/scatter-add | solution.py:31
  38.3 4.5 %collective-permute-start.11 = (bf16[2,32,128]{2,1,0:T(8,128)(2,1)S(1)}, bf16[2,32,128]{2,1,0:T(8,128)(2,1)S(1)}, u32[]{:S(2)}, u32[]{:S(2)}) collective-permute-start(bf16[2,32,128]{2,1,0:T(8,128)(2,1)S(1)} %collective-permute-done.10), channel_id=1, source_target_pairs={{0,15},{1,0},{2,1},{3,2},{4,3},{5,4},{6,5},{7,6},{8,7},{9,8},{10,9... | collective-permute-start | bytes 49160 | tf_op jit(solution)/shard_map/ppermute | solution.py:89
  42.9 1.3 %collective-permute-done.11 = bf16[2,32,128]{2,1,0:T(8,128)(2,1)S(1)} collective-permute-done((bf16[2,32,128]{2,1,0:T(8,128)(2,1)S(1)}, bf16[2,32,128]{2,1,0:T(8,128)(2,1)S(1)}, u32[]{:S(2)}, u32[]{:S(2)}) %collective-permute-start.11) | collective-permute-done | bytes 16416 | tf_op jit(solution)/shard_map/ppermute | solution.py:89
  44.3 4.4 %collective-permute-start.12 = (bf16[2,32,128]{2,1,0:T(8,128)(2,1)S(1)}, bf16[2,32,128]{2,1,0:T(8,128)(2,1)S(1)}, u32[]{:S(2)}, u32[]{:S(2)}) collective-permute-start(bf16[2,32,128]{2,1,0:T(8,128)(2,1)S(1)} %collective-permute-done.11), channel_id=1, source_target_pairs={{0,15},{1,0},{2,1},{3,2},{4,3},{5,4},{6,5},{7,6},{8,7},{9,8},{10,9... | collective-permute-start | bytes 49160 | tf_op jit(solution)/shard_map/ppermute | solution.py:89
  49.0 1.1 %collective-permute-done.12 = bf16[2,32,128]{2,1,0:T(8,128)(2,1)S(1)} collective-permute-done((bf16[2,32,128]{2,1,0:T(8,128)(2,1)S(1)}, bf16[2,32,128]{2,1,0:T(8,128)(2,1)S(1)}, u32[]{:S(2)}, u32[]{:S(2)}) %collective-permute-start.12) | collective-permute-done | bytes 16416 | tf_op jit(solution)/shard_map/ppermute | solution.py:89
  50.1 4.4 %collective-permute-start.13 = (bf16[2,32,128]{2,1,0:T(8,128)(2,1)S(1)}, bf16[2,32,128]{2,1,0:T(8,128)(2,1)S(1)}, u32[]{:S(2)}, u32[]{:S(2)}) collective-permute-start(bf16[2,32,128]{2,1,0:T(8,128)(2,1)S(1)} %collective-permute-done.12), channel_id=1, source_target_pairs={{0,15},{1,0},{2,1},{3,2},{4,3},{5,4},{6,5},{7,6},{8,7},{9,8},{10,9... | collective-permute-start | bytes 49160 | tf_op jit(solution)/shard_map/ppermute | solution.py:89
  54.9 1.1 %collective-permute-done.13 = bf16[2,32,128]{2,1,0:T(8,128)(2,1)S(1)} collective-permute-done((bf16[2,32,128]{2,1,0:T(8,128)(2,1)S(1)}, bf16[2,32,128]{2,1,0:T(8,128)(2,1)S(1)}, u32[]{:S(2)}, u32[]{:S(2)}) %collective-permute-start.13) | collective-permute-done | bytes 16416 | tf_op jit(solution)/shard_map/ppermute | solution.py:89
  56.0 4.4 %collective-permute-start.14 = (bf16[2,32,128]{2,1,0:T(8,128)(2,1)S(1)}, bf16[2,32,128]{2,1,0:T(8,128)(2,1)S(1)}, u32[]{:S(2)}, u32[]{:S(2)}) collective-permute-start(bf16[2,32,128]{2,1,0:T(8,128)(2,1)S(1)} %collective-permute-done.13), channel_id=1, source_target_pairs={{0,15},{1,0},{2,1},{3,2},{4,3},{5,4},{6,5},{7,6},{8,7},{9,8},{10,9... | collective-permute-start | bytes 49160 | tf_op jit(solution)/shard_map/ppermute | solution.py:89
  60.8 0.7 constant_dynamic-update-slice_fusion.23
  61.9 0.7 constant_dynamic-update-slice_fusion.7
  62.8 7.6 %gather_fusion = bf16[2048,128]{1,0:T(8,128)(2,1)S(1)} fusion(bf16[8192,128]{1,0:T(8,128)(2,1)} %all-gather.2.cloned.1.call-done, s32[2048]{0:T(1024)S(1)} %broadcast_clamp_fusion), kind=kCustom, calls=%fused_computation | custom fusion | bytes 1056768 | tf_op jit(solution)/shard_map/jit(_take)/gather | solution.py:71
  70.4 0.9 multiply_reduce_fusion
  73.6 0.7 reshape.153
  74.4 5.8 %all-to-all-start = ((f32[16,1,1024]{2,1,0:T(1,128)}), f32[16,1,1024]{2,1,0:T(1,128)S(1)}, u32[]{:S(2)}, u32[]{:S(2)}) async-start(f32[16,1,1024]{2,1,0:T(1,128)} %reshape.153), calls=%async_computation | async-start | bytes 131072 | tf_op jit(solution)/shard_map/all_to_all | solution.py:102
  80.3 6.9 %gather_fusion.1 = s32[1024]{0:T(1024)S(1)} fusion(s32[160]{0:T(256)S(1)} %get-tuple-element.6, s32[1024]{0:T(1024)S(1)} %broadcast_clamp_fusion.1), kind=kCustom, calls=%fused_computation.1 | custom fusion | bytes 12288 | tf_op jit(solution)/shard_map/gather | solution.py:40
  87.8 0.8 reduce.8
  89.6 4.0 %fusion.3 = f32[2,256]{0,1:T(8,128)S(1)} fusion(f32[2,32,256]{1,0,2:T(2,128)S(1)} %all_to_all.19, f32[2,32,1]{1,0,2:T(2,128)S(1)} %concatenate.35, f32[2,32,255]{1,0,2:T(2,128)S(1)} %copy.29, f32[2,32,2]{1,0,2:T(2,128)S(1)} %concatenate.39, f32[2,32,254]{1,0,2:T(2,128)S(1)} %copy.31, pred[256]{0:T(512)(128)(4,1)S(1)} %concatenate.37, ...), kind=kLoop, calls=%fused_computation.20 | loop fusion | flops 114176 | bytes 199168 | tf_op jit(solution)/shard_map/qit,qct->qc/reduce_sum | solution.py:44
  (108 shorter events, 14.2 us)
Async XLA Ops:
  6.5 56.3 %all-gather.2.cloned.1.call-start = ((), (), s32[]{:S(2)}) async-start(), calls=%async_computation.1 | async-start | bytes 2228224 | tf_op jit(solution)/shard_map/all_gather | solution.py:70
  6.5 11.0 %collective-permute-start = (bf16[2,32,128]{2,1,0:T(8,128)(2,1)}, bf16[2,32,128]{2,1,0:T(8,128)(2,1)S(1)}, u32[]{:S(2)}, u32[]{:S(2)}) collective-permute-start(bf16[2,32,128]{2,1,0:T(8,128)(2,1)} %param.9), channel_id=1, source_target_pairs={{0,1},{1,2},{2,3},{3,4},{4,5},{5,6},{6,7},{7,8},{8,9},{9,10},{10,1... | collective-permute-start | bytes 49160 | tf_op jit(solution)/shard_map/ppermute | solution.py:87
  7.0 17.2 %collective-permute-start.8 = (bf16[2,32,128]{2,1,0:T(8,128)(2,1)}, bf16[2,32,128]{2,1,0:T(8,128)(2,1)S(1)}, u32[]{:S(2)}, u32[]{:S(2)}) collective-permute-start(bf16[2,32,128]{2,1,0:T(8,128)(2,1)} %param.9), channel_id=1, source_target_pairs={{0,15},{1,0},{2,1},{3,2},{4,3},{5,4},{6,5},{7,6},{8,7},{9,8},{10,9... | collective-permute-start | bytes 49160 | tf_op jit(solution)/shard_map/ppermute | solution.py:89
  17.5 6.0 %collective-permute-start.1 = (bf16[2,32,128]{2,1,0:T(8,128)(2,1)S(1)}, bf16[2,32,128]{2,1,0:T(8,128)(2,1)S(1)}, u32[]{:S(2)}, u32[]{:S(2)}) collective-permute-start(bf16[2,32,128]{2,1,0:T(8,128)(2,1)S(1)} %collective-permute-done), channel_id=1, source_target_pairs={{0,1},{1,2},{2,3},{3,4},{4,5},{5,6},{6,7},{7,8},{8,9},{9,10},{10,1... | collective-permute-start | bytes 49160 | tf_op jit(solution)/shard_map/ppermute | solution.py:87
  23.5 6.0 %collective-permute-start.2 = (bf16[2,32,128]{2,1,0:T(8,128)(2,1)S(1)}, bf16[2,32,128]{2,1,0:T(8,128)(2,1)S(1)}, u32[]{:S(2)}, u32[]{:S(2)}) collective-permute-start(bf16[2,32,128]{2,1,0:T(8,128)(2,1)S(1)} %collective-permute-done.1), channel_id=1, source_target_pairs={{0,1},{1,2},{2,3},{3,4},{4,5},{5,6},{6,7},{7,8},{8,9},{9,10},{10,1... | collective-permute-start | bytes 49160 | tf_op jit(solution)/shard_map/ppermute | solution.py:87
  24.2 5.9 %collective-permute-start.9 = (bf16[2,32,128]{2,1,0:T(8,128)(2,1)S(1)}, bf16[2,32,128]{2,1,0:T(8,128)(2,1)S(1)}, u32[]{:S(2)}, u32[]{:S(2)}) collective-permute-start(bf16[2,32,128]{2,1,0:T(8,128)(2,1)S(1)} %collective-permute-done.8), channel_id=1, source_target_pairs={{0,15},{1,0},{2,1},{3,2},{4,3},{5,4},{6,5},{7,6},{8,7},{9,8},{10,9... | collective-permute-start | bytes 49160 | tf_op jit(solution)/shard_map/ppermute | solution.py:89
  29.5 5.9 %collective-permute-start.3 = (bf16[2,32,128]{2,1,0:T(8,128)(2,1)S(1)}, bf16[2,32,128]{2,1,0:T(8,128)(2,1)S(1)}, u32[]{:S(2)}, u32[]{:S(2)}) collective-permute-start(bf16[2,32,128]{2,1,0:T(8,128)(2,1)S(1)} %collective-permute-done.2), channel_id=1, source_target_pairs={{0,1},{1,2},{2,3},{3,4},{4,5},{5,6},{6,7},{7,8},{8,9},{9,10},{10,1... | collective-permute-start | bytes 49160 | tf_op jit(solution)/shard_map/ppermute | solution.py:87
  30.2 8.2 %collective-permute-start.10 = (bf16[2,32,128]{2,1,0:T(8,128)(2,1)S(1)}, bf16[2,32,128]{2,1,0:T(8,128)(2,1)S(1)}, u32[]{:S(2)}, u32[]{:S(2)}) collective-permute-start(bf16[2,32,128]{2,1,0:T(8,128)(2,1)S(1)} %collective-permute-done.9), channel_id=1, source_target_pairs={{0,15},{1,0},{2,1},{3,2},{4,3},{5,4},{6,5},{7,6},{8,7},{9,8},{10,9... | collective-permute-start | bytes 49160 | tf_op jit(solution)/shard_map/ppermute | solution.py:89
  35.4 7.4 %collective-permute-start.4 = (bf16[2,32,128]{2,1,0:T(8,128)(2,1)S(1)}, bf16[2,32,128]{2,1,0:T(8,128)(2,1)S(1)}, u32[]{:S(2)}, u32[]{:S(2)}) collective-permute-start(bf16[2,32,128]{2,1,0:T(8,128)(2,1)S(1)} %collective-permute-done.3), channel_id=1, source_target_pairs={{0,1},{1,2},{2,3},{3,4},{4,5},{5,6},{6,7},{7,8},{8,9},{9,10},{10,1... | collective-permute-start | bytes 49160 | tf_op jit(solution)/shard_map/ppermute | solution.py:87
  38.3 5.9 %collective-permute-start.11 = (bf16[2,32,128]{2,1,0:T(8,128)(2,1)S(1)}, bf16[2,32,128]{2,1,0:T(8,128)(2,1)S(1)}, u32[]{:S(2)}, u32[]{:S(2)}) collective-permute-start(bf16[2,32,128]{2,1,0:T(8,128)(2,1)S(1)} %collective-permute-done.10), channel_id=1, source_target_pairs={{0,15},{1,0},{2,1},{3,2},{4,3},{5,4},{6,5},{7,6},{8,7},{9,8},{10,9... | collective-permute-start | bytes 49160 | tf_op jit(solution)/shard_map/ppermute | solution.py:89
  42.8 6.1 %collective-permute-start.5 = (bf16[2,32,128]{2,1,0:T(8,128)(2,1)S(1)}, bf16[2,32,128]{2,1,0:T(8,128)(2,1)S(1)}, u32[]{:S(2)}, u32[]{:S(2)}) collective-permute-start(bf16[2,32,128]{2,1,0:T(8,128)(2,1)S(1)} %collective-permute-done.4), channel_id=1, source_target_pairs={{0,1},{1,2},{2,3},{3,4},{4,5},{5,6},{6,7},{7,8},{8,9},{9,10},{10,1... | collective-permute-start | bytes 49160 | tf_op jit(solution)/shard_map/ppermute | solution.py:87
  44.3 5.9 %collective-permute-start.12 = (bf16[2,32,128]{2,1,0:T(8,128)(2,1)S(1)}, bf16[2,32,128]{2,1,0:T(8,128)(2,1)S(1)}, u32[]{:S(2)}, u32[]{:S(2)}) collective-permute-start(bf16[2,32,128]{2,1,0:T(8,128)(2,1)S(1)} %collective-permute-done.11), channel_id=1, source_target_pairs={{0,15},{1,0},{2,1},{3,2},{4,3},{5,4},{6,5},{7,6},{8,7},{9,8},{10,9... | collective-permute-start | bytes 49160 | tf_op jit(solution)/shard_map/ppermute | solution.py:89
  48.9 5.9 %collective-permute-start.6 = (bf16[2,32,128]{2,1,0:T(8,128)(2,1)S(1)}, bf16[2,32,128]{2,1,0:T(8,128)(2,1)S(1)}, u32[]{:S(2)}, u32[]{:S(2)}) collective-permute-start(bf16[2,32,128]{2,1,0:T(8,128)(2,1)S(1)} %collective-permute-done.5), channel_id=1, source_target_pairs={{0,1},{1,2},{2,3},{3,4},{4,5},{5,6},{6,7},{7,8},{8,9},{9,10},{10,1... | collective-permute-start | bytes 49160 | tf_op jit(solution)/shard_map/ppermute | solution.py:87
  50.1 5.9 %collective-permute-start.13 = (bf16[2,32,128]{2,1,0:T(8,128)(2,1)S(1)}, bf16[2,32,128]{2,1,0:T(8,128)(2,1)S(1)}, u32[]{:S(2)}, u32[]{:S(2)}) collective-permute-start(bf16[2,32,128]{2,1,0:T(8,128)(2,1)S(1)} %collective-permute-done.12), channel_id=1, source_target_pairs={{0,15},{1,0},{2,1},{3,2},{4,3},{5,4},{6,5},{7,6},{8,7},{9,8},{10,9... | collective-permute-start | bytes 49160 | tf_op jit(solution)/shard_map/ppermute | solution.py:89
  54.8 5.9 %collective-permute-start.7 = (bf16[2,32,128]{2,1,0:T(8,128)(2,1)S(1)}, bf16[2,32,128]{2,1,0:T(8,128)(2,1)S(1)}, u32[]{:S(2)}, u32[]{:S(2)}) collective-permute-start(bf16[2,32,128]{2,1,0:T(8,128)(2,1)S(1)} %collective-permute-done.6), channel_id=1, source_target_pairs={{0,1},{1,2},{2,3},{3,4},{4,5},{5,6},{6,7},{7,8},{8,9},{9,10},{10,1... | collective-permute-start | bytes 49160 | tf_op jit(solution)/shard_map/ppermute | solution.py:87
  56.0 5.9 %collective-permute-start.14 = (bf16[2,32,128]{2,1,0:T(8,128)(2,1)S(1)}, bf16[2,32,128]{2,1,0:T(8,128)(2,1)S(1)}, u32[]{:S(2)}, u32[]{:S(2)}) collective-permute-start(bf16[2,32,128]{2,1,0:T(8,128)(2,1)S(1)} %collective-permute-done.13), channel_id=1, source_target_pairs={{0,15},{1,0},{2,1},{3,2},{4,3},{5,4},{6,5},{7,6},{8,7},{9,8},{10,9... | collective-permute-start | bytes 49160 | tf_op jit(solution)/shard_map/ppermute | solution.py:89
  62.8 7.6 %copy-start = (s32[2048,128]{1,0:T(8,128)S(1)}, s32[2048,128]{1,0:T(8,128)}, u32[]{:S(2)}) copy-start(s32[2048,128]{1,0:T(8,128)} %param.15) | copy-start | bytes 3145732
  74.4 12.9 %all-to-all-start = ((f32[16,1,1024]{2,1,0:T(1,128)}), f32[16,1,1024]{2,1,0:T(1,128)S(1)}, u32[]{:S(2)}, u32[]{:S(2)}) async-start(f32[16,1,1024]{2,1,0:T(1,128)} %reshape.153), calls=%async_computation | async-start | bytes 131072 | tf_op jit(solution)/shard_map/all_to_all | solution.py:102
Sparse Core Ops, SparseCore 0:
  12.2 42.3 all-gather.1
